TPU v7x, 32 devices: a whole 2x2x4 slice. The times are simulated.
32 devices in a mesh: dom: 16 (over z, y, core), feat: 2 (over x).
Axes of the slice: x: 2, y: 2, z: 4, core: 2. Of those that a mesh axis runs over, the one named last changes fastest.
Arguments:
- features: bfloat16 [256, 8192], P('feat', 'dom'), may hold values from -6 to 6
- in_degree: int32 [8192], P('dom'), may hold values from 16 to 64
- send_rows: int32 [16, 16, 16], P('dom'), may hold values from 0 to 511
- send_count: int32 [16, 16], P('dom'), may hold values from 0 to 16, as said below
- hub_owner: int32 [4], replicated, may hold values from 0 to 15, as said below
- hub_rows: int32 [4, 128], replicated, may hold values from 0 to 511
- local_dest: int32 [256], P('dom'), may hold values from 0 to 3
- local_source: int32 [256], P('dom'), may hold values from 0 to 3
- local_tiles: bfloat16 [256, 128, 128], P('dom'), may hold values from 0 to 1
- border_dest: int32 [256], P('dom'), may hold values from 0 to 3
- border_source: int32 [256], P('dom'), may hold values from 0 to 1
- border_tiles: bfloat16 [256, 128, 128], P('dom'), may hold values from 0 to 1
- hub_dest: int32 [256], P('dom'), may hold values from 0 to 3
- hub_source: int32 [256], P('dom'), may hold values from 0 to 3
- hub_tiles: bfloat16 [256, 128, 128], P('dom'), may hold values from 0 to 1
- self_weight: bfloat16 [256, 256], P('feat'), may hold values from -0.375 to 0.375
- neighbor_weight: bfloat16 [256, 256], P('feat'), may hold values from -0.375 to 0.375
- out_bias: float32 [256], P('feat'), may hold values from -3 to 3
Outputs:
- updated: bfloat16 [256, 8192], P('feat', 'dom')
Inputs may be any that keep to these rules, and one draw needn't show every extreme that they name: send_count[q, p] of the 16 slots from q to p are live; in every draw some destinations receive 16 live rows from every source. Hub block b belongs to partition hub_owner[b]; one partition owns exactly 2 blocks, every other partition at most one.
All inputs are finite; a program needn't handle non-finite values.
Results may differ from a plain program's by a relative error of at most 0.0034.
Values may be sent and summed in bfloat16 or wider, within the bound.
No kernel may reach another device: no remote copies, remote signals or barrier semaphores. Data moves between devices by JAX's collectives and lax.ppermute only.
A program may use at most 64 MiB of HBM per device.

v0:
```python
import jax
import jax.numpy as jnp
from jax import lax
from jax.sharding import PartitionSpec as P

HOWN = 2


def tile_terms(blocks, targets, source, tile_values, row_blocks):
    picked = jnp.take(blocks, source, axis=1)
    partial_value = jnp.einsum(
        "ftk,tik->fti", picked, tile_values, preferred_element_type=jnp.float32
    )
    onehot = (targets[:, None] == jnp.arange(row_blocks, dtype=jnp.int32)[None, :]).astype(
        jnp.float32
    )
    return jnp.einsum("fti,tr->fri", partial_value, onehot, precision=lax.Precision.HIGHEST)


def shards(
    features,
    in_degree,
    send_rows,
    send_count,
    hub_owner,
    hub_rows,
    local_dest,
    local_source,
    local_tiles,
    border_dest,
    border_source,
    border_tiles,
    hub_dest,
    hub_source,
    hub_tiles,
    self_weight,
    neighbor_weight,
    out_bias,
):
    feat_rows, vertex_count = features.shape
    tile_size = local_tiles.shape[1]
    row_blocks = vertex_count // tile_size
    partitions = lax.axis_size("dom")
    capacity = send_rows.shape[2]
    own_blocks = features.reshape(feat_rows, row_blocks, tile_size)
    local_sum = tile_terms(own_blocks, local_dest, local_source, local_tiles, row_blocks)
    pick_rows = send_rows[0].reshape(-1)
    outgoing = jnp.take(features, pick_rows, axis=1).reshape(feat_rows, partitions, capacity)
    alive_slots = (jnp.arange(capacity, dtype=jnp.int32)[None, :] < send_count[0][:, None]).astype(
        jnp.bfloat16
    )
    outgoing = outgoing * alive_slots[None]
    incoming = lax.all_to_all(outgoing, "dom", split_axis=1, concat_axis=1, tiled=True)
    border_blocks = incoming.reshape(feat_rows, partitions * capacity // tile_size, tile_size)
    border_sum = tile_terms(border_blocks, border_dest, border_source, border_tiles, row_blocks)
    hub_count = hub_owner.shape[0]
    position = lax.axis_index("dom")
    block_ids = jnp.arange(hub_count, dtype=jnp.int32)
    earlier = block_ids[:, None] > block_ids[None, :]
    same_owner = hub_owner[:, None] == hub_owner[None, :]
    order_rank = jnp.sum((earlier & same_owner).astype(jnp.int32), axis=1)
    owned_here = hub_owner == position
    choose = (
        owned_here[None, :] & (order_rank[None, :] == jnp.arange(HOWN, dtype=jnp.int32)[:, None])
    ).astype(jnp.int32)
    slot_rows = jnp.sum(choose[:, :, None] * hub_rows[None], axis=1)
    owned_blocks = jnp.take(features, slot_rows.reshape(-1), axis=1).reshape(
        feat_rows, HOWN, tile_size
    )
    everyone = lax.all_gather(owned_blocks, "dom", axis=1, tiled=True)
    hub_blocks = jnp.take(everyone, hub_owner * HOWN + order_rank, axis=1)
    hub_sum = tile_terms(hub_blocks, hub_dest, hub_source, hub_tiles, row_blocks)
    degree = in_degree.astype(jnp.float32).reshape(row_blocks, tile_size)
    aggregate = (
        ((local_sum + border_sum + hub_sum) / degree[None])
        .astype(jnp.bfloat16)
        .reshape(feat_rows, vertex_count)
    )
    running = jnp.dot(
        self_weight,
        lax.all_gather(features, "feat", axis=0, tiled=True),
        preferred_element_type=jnp.float32,
    )
    combined = running + jnp.dot(
        neighbor_weight,
        lax.all_gather(aggregate, "feat", axis=0, tiled=True),
        preferred_element_type=jnp.float32,
    )
    return jnp.maximum(combined + out_bias[:, None], 0.0).astype(jnp.bfloat16)


def solution(mesh):
    placed = (
        P("feat", "dom"),
        P("dom"),
        P("dom", None, None),
        P("dom", None),
        P(),
        P(),
        P("dom"),
        P("dom"),
        P("dom", None, None),
        P("dom"),
        P("dom"),
        P("dom", None, None),
        P("dom"),
        P("dom"),
        P("dom", None, None),
        P("feat", None),
        P("feat", None),
        P("feat"),
    )
    return jax.shard_map(
        shards, mesh=mesh, in_specs=placed, out_specs=P("feat", "dom"), check_vma=False
    )
```

profile of v0, /device:TPU:0, one launch (start us, length us, event | category | flops | bytes accessed | tf_op | source)
XLA Modules:
  0.0 80.8 jit_solution(9627374421501627303)
XLA Ops:
  6.5 0.8 %reshape_squeeze.3 = s32[256]{0:T(256)S(1)} reshape(s32[1,16,16]{2,1,0:T(8,128)} %param.24) | data formatting | bytes 2048 | tf_op jit(solution)/shard_map/reshape;squeeze | solution.py:47
  7.4 1.0 %copy.61 = bf16[128,512]{0,1:T(8,128)(2,1)S(1)} copy(bf16[128,512]{1,0:T(8,128)(2,1)} %param.22) | data formatting | bytes 262144 | tf_op args[0]
  8.4 0.6 copy-done.11
  9.2 0.9 %gather_fusion.3 = bf16[256,128]{1,0:T(8,128)(2,1)S(1)} fusion(bf16[128,512]{0,1:T(8,128)(2,1)S(1)} %copy.61, s32[1024]{0:T(1024)S(1)} %pad_clamp_fusion.4), kind=kCustom, calls=%fused_computation.1.clone | custom fusion | bytes 132096 | tf_op jit(solution)/shard_map/jit(_take)/gather | solution.py:48
  10.1 0.7 broadcast_multiply_fusion
  10.9 7.4 %all-to-all-start = ((bf16[128,16,16]{0,2,1:T(8,128)(2,1)}), bf16[128,16,16]{0,2,1:T(8,128)(2,1)S(1)}, u32[]{:S(2)}, u32[]{:S(2)}) async-start(bf16[128,16,16]{0,2,1:T(8,128)(2,1)} %broadcast_multiply_fusion), calls=%async_computation | async-start | bytes 131072 | tf_op jit(solution)/shard_map/all_to_all | solution.py:53
  18.3 0.6 copy-done.12
  18.9 0.2 convert_reduce_fusion
  19.1 0.7 copy-done.6
  19.9 0.9 %gather_fusion.4 = bf16[256,128]{1,0:T(8,128)(2,1)S(1)} fusion(bf16[128,512]{0,1:T(8,128)(2,1)S(1)} %copy.61, s32[1024]{0:T(1024)S(1)} %pad_clamp_fusion.2), kind=kCustom, calls=%fused_computation.3.clone | custom fusion | bytes 132096 | tf_op jit(solution)/shard_map/jit(_take)/gather | solution.py:67
  20.9 0.7 copy.68
  21.6 0.6 copy-done.13
  22.3 0.6 copy-done.14
  23.1 0.6 gather_fusion.2
  23.8 0.6 copy-done.7
  24.5 0.5 convolution_bitcast_fusion.2
  25.1 1.1 %fusion.7 = f32[4,128,128]{2,0,1:T(4,128)S(1)} fusion(f32[128,16,128]{2,0,1:T(8,128)S(1)} %convolution_bitcast_fusion.2, s32[16]{0:T(128)S(1)} %copy-done.8), kind=kOutput, calls=%fused_computation.20 | convolution fusion | flops 12582976 | bytes 1310784 | tf_op jit(solution)/shard_map/fti,tr->fri/dot_general | solution.py:17
  26.2 6.5 %all_gather.9 = bf16[256,512]{1,0:T(8,128)(2,1)S(1)} all-gather(bf16[128,512]{1,0:T(8,128)(2,1)S(1)} %copy-done.3), channel_id=1, replica_groups=mesh['dom'=16,'feat'=2] {'feat'}, dimensions={0}, use_global_device_ids=true | all-gather | bytes 393216 | tf_op jit(solution)/shard_map/all_gather | solution.py:81
  32.9 0.6 gather_fusion
  33.5 0.4 copy-done.1
  33.9 0.5 convolution_bitcast_fusion.1
  34.6 1.1 %convolution_add_fusion.1 = f32[4,128,128]{2,0,1:T(4,128)S(1)} fusion(f32[4,128,128]{2,0,1:T(4,128)S(1)} %fusion.7, f32[128,16,128]{2,0,1:T(8,128)S(1)} %convolution_bitcast_fusion.1, s32[16]{0:T(128)S(1)} %copy-done.9), kind=kOutput, calls=%fused_computation.10 | convolution fusion | flops 12648512 | bytes 1572928 | tf_op jit(solution)/shard_map/fti,tr->fri/dot_general | solution.py:17
  35.6 25.4 %all-gather.2.cloned.1.call-done = bf16[128,32,128]{2,0,1:T(8,128)(2,1)} async-done(((bf16[128,2,128]{2,0,1:T(8,128)(2,1)}), bf16[128,32,128]{2,0,1:T(8,128)(2,1)}) %all-gather.2.cloned.1.call-update) | async-done | bytes 1048592 | tf_op jit(solution)/shard_map/all_gather | solution.py:70
  61.0 1.8 %gather_fusion.1 = bf16[4,128,128]{2,1,0:T(8,128)(2,1)S(1)} fusion(bf16[128,32,128]{2,0,1:T(8,128)(2,1)} %all-gather.2.cloned.1.call-done, s32[1024]{0:T(1024)S(1)} %pad_clamp_fusion.1), kind=kCustom, calls=%fused_computation.5 | custom fusion | bytes 262160 | tf_op jit(solution)/shard_map/jit(_take)/gather | solution.py:71
  62.9 0.6 gather_fusion.5
  63.6 0.4 copy-done.2
  64.0 0.5 convolution_bitcast_fusion
  64.6 1.1 %fusion.3 = bf16[4,128,128]{2,0,1:T(4,128)(2,1)S(1)} fusion(f32[4,128,128]{2,0,1:T(4,128)S(1)} %convolution_add_fusion.1, f32[128,16,128]{2,0,1:T(8,128)S(1)} %convolution_bitcast_fusion, f32[4,128]{1,0:T(4,128)S(1)} %convert_bitcast_fusion, s32[16]{0:T(128)S(1)} %copy-done.16), kind=kOutput, calls=%fused_computation.16 | convolution fusion | flops 12779584 | bytes 1443904 | tf_op jit(solution)/shard_map/fti,tr->fri/dot_general | solution.py:17
  65.7 6.5 %all_gather.11 = bf16[256,512]{1,0:T(8,128)(2,1)S(1)} all-gather(bf16[128,512]{1,0:T(8,128)(2,1)S(1)} %bitcast.56), channel_id=1, replica_groups=mesh['dom'=16,'feat'=2] {'feat'}, dimensions={0}, use_global_device_ids=true | all-gather | bytes 393216 | tf_op jit(solution)/shard_map/all_gather | solution.py:86
  72.2 0.2 convolution_bitcast_fusion.3
  72.4 0.6 copy-done.5
  73.1 0.8 %fusion.4 = bf16[128,512]{1,0:T(8,128)(2,1)} fusion(f32[128,512]{1,0:T(8,128)S(1)} %convolution_bitcast_fusion.3, bf16[128,256]{1,0:T(8,128)(2,1)S(1)} %copy-done.5, bf16[256,512]{1,0:T(8,128)(2,1)S(1)} %all_gather.9, f32[128]{0:T(128)S(1)} %copy-done.10), kind=kOutput, calls=%fused_computation.17 | convolution fusion | flops 33816576 | bytes 721408 | tf_op jit(solution)/shard_map/dot_general | solution.py:79
  (55 shorter events, 1.3 us)
Async XLA Ops:
  6.5 17.9 %copy-start = (bf16[16,128,128]{2,1,0:T(8,128)(2,1)S(1)}, bf16[16,128,128]{2,1,0:T(8,128)(2,1)}, u32[]{:S(2)}) copy-start(bf16[16,128,128]{2,1,0:T(8,128)(2,1)} %param.30) | copy-start | bytes 1572868
  8.4 0.7 copy-start.11
  10.9 21.9 %all-to-all-start = ((bf16[128,16,16]{0,2,1:T(8,128)(2,1)}), bf16[128,16,16]{0,2,1:T(8,128)(2,1)S(1)}, u32[]{:S(2)}, u32[]{:S(2)}) async-start(bf16[128,16,16]{0,2,1:T(8,128)(2,1)} %broadcast_multiply_fusion), calls=%async_computation | async-start | bytes 131072 | tf_op jit(solution)/shard_map/all_to_all | solution.py:53
  18.3 0.7 copy-start.12
  18.3 42.8 %all-gather.2.cloned.1.call-start = ((), (), s32[]{:S(2)}) async-start(), calls=%async_computation.1 | async-start | bytes 1114112 | tf_op jit(solution)/shard_map/all_gather | solution.py:70
  19.1 0.7 copy-start.6
  21.6 0.7 copy-start.13
  22.3 0.7 copy-start.14
  23.1 0.7 copy-start.15
  23.8 0.7 copy-start.7
  24.5 0.7 copy-start.8
  25.1 1.1 %copy-start.3 = (bf16[128,512]{1,0:T(8,128)(2,1)S(1)}, bf16[128,512]{1,0:T(8,128)(2,1)}, u32[]{:S(2)}) copy-start(bf16[128,512]{1,0:T(8,128)(2,1)} %param.22) | copy-start | bytes 393220
  32.9 1.0 %copy-start.1 = (bf16[16,128,128]{2,1,0:T(8,128)(2,1)S(1)}, bf16[16,128,128]{2,1,0:T(8,128)(2,1)}, u32[]{:S(2)}) copy-start(bf16[16,128,128]{2,1,0:T(8,128)(2,1)} %param.33) | copy-start | bytes 1572868
  33.9 0.7 copy-start.9
  62.9 1.0 %copy-start.2 = (bf16[16,128,128]{2,1,0:T(8,128)(2,1)S(1)}, bf16[16,128,128]{2,1,0:T(8,128)(2,1)}, u32[]{:S(2)}) copy-start(bf16[16,128,128]{2,1,0:T(8,128)(2,1)} %param.36) | copy-start | bytes 1572868
  64.0 0.7 copy-start.16
  65.7 6.5 %copy-start.4 = (bf16[128,256]{1,0:T(8,128)(2,1)S(1)}, bf16[128,256]{1,0:T(8,128)(2,1)}, u32[]{:S(2)}) copy-start(bf16[128,256]{1,0:T(8,128)(2,1)} %param.38) | copy-start | bytes 196612
  72.2 0.8 %copy-start.5 = (bf16[128,256]{1,0:T(8,128)(2,1)S(1)}, bf16[128,256]{1,0:T(8,128)(2,1)}, u32[]{:S(2)}) copy-start(bf16[128,256]{1,0:T(8,128)(2,1)} %param.37) | copy-start | bytes 196612
  72.2 0.8 %copy-start.10 = (f32[128]{0:T(128)S(1)}, f32[128]{0:T(128)}, u32[]{:S(2)}) copy-start(f32[128]{0:T(128)} %param.39) | copy-start | bytes 1540
Sparse Core Ops, SparseCore 0:
  21.7 39.2 all-gather.1
where the time goes:
time: 81.3 us; the launch traced here: 80.8 us
  waiting for transfers between devices  25.4 us (31%)
  local copies, waits for them, and re-layouts  14 us (17%)
  between operations  13.7 us (17%)
  blocking collectives  13 us (16%)
  starting transfers between devices  7.43 us (9%)
  matrix products  5.75 us (7%)
  other arithmetic  1.48 us (2%)
    all_gather x1, waiting for transfers between devices, shards(): everyone = lax.all_gather(owned_blocks, 'dom', axis=1, tiled=True)  25.4 us
    all_to_all x1, starting transfers between devices, shards(): lax.all_to_all(outgoing, 'dom', split_axis=1, concat_axis=1, tiled=True)  7.38 us
    unnamed x36, local copies, waits for them, and re-layouts  6.71 us
    all_gather x1, blocking collectives, shards(): lax.all_gather(features, 'feat', axis=0, tiled=True)  6.51 us
    all_gather x1, blocking collectives, shards(): lax.all_gather(aggregate, 'feat', axis=0, tiled=True)  6.47 us
    dot_general x3, matrix products, tile_terms(): jnp.einsum('fti,tr->fri', partial_value, onehot, precision=lax.Precision....  3.16 us
    gather x3, local copies, waits for them, and re-layouts, tile_terms(): picked = jnp.take(blocks, source, axis=1)  1.94 us
    gather x1, local copies, waits for them, and re-layouts, shards(): hub_blocks = jnp.take(everyone, hub_owner * HOWN + order_rank, axis=1)  1.79 us
  transfers between devices with their start and end apart: 2, of which 1 were waited for; matrix products, arithmetic and copies ran while one was open for 8% of the time, Pallas kernels for 0%

commit v1 on v0

--- a/solution.py
+++ b/solution.py
@@ -4,6 +4,19 @@
 from jax.sharding import PartitionSpec as P
 
 HOWN = 2
+
+
+def ring_gather(value, axis, dim):
+    ways = lax.axis_size(axis)
+    up = [(d, (d + 1) % ways) for d in range(ways)]
+    down = [(d, (d - 1) % ways) for d in range(ways)]
+    earlier, later = ([value], [value])
+    for _ in range(ways // 2):
+        earlier.append(lax.ppermute(earlier[-1], axis, up))
+    for _ in range((ways - 1) // 2):
+        later.append(lax.ppermute(later[-1], axis, down))
+    line = jnp.concatenate([*earlier[::-1], *later[1:]], axis=dim)
+    return jnp.roll(line, (lax.axis_index(axis) - ways // 2) * value.shape[dim], axis=dim)
 
 
 def tile_terms(blocks, targets, source, tile_values, row_blocks):
@@ -67,7 +80,7 @@
     owned_blocks = jnp.take(features, slot_rows.reshape(-1), axis=1).reshape(
         feat_rows, HOWN, tile_size
     )
-    everyone = lax.all_gather(owned_blocks, "dom", axis=1, tiled=True)
+    everyone = ring_gather(owned_blocks, "dom", 1)
     hub_blocks = jnp.take(everyone, hub_owner * HOWN + order_rank, axis=1)
     hub_sum = tile_terms(hub_blocks, hub_dest, hub_source, hub_tiles, row_blocks)
     degree = in_degree.astype(jnp.float32).reshape(row_blocks, tile_size)

time: 81.3 us -> 81.7 us (level)
  starting transfers between devices: 7.43 us -> 35.7 us
  between operations: 13.7 us -> 0.58 us
  waiting for transfers between devices: 25.4 us -> 15.5 us
  local copies, waits for them, and re-layouts: 14 us -> 7.06 us
  other arithmetic: 1.48 us -> 5.5 us
  blocking collectives: 13 us -> 11.3 us
    ppermute x0 -> x15, starting transfers between devices: none -> 32.1 us  [the longest x7 31.1 us: ring_gather(): later.append(lax.ppermute(later[-1], axis, down))]
    all_gather x1 -> x0, waiting for transfers between devices: 25.4 us -> none  [shards(): everyone = lax.all_gather(owned_blocks, 'dom', axis=1, tiled=True)]
    ppermute x0 -> x15, waiting for transfers between devices: none -> 15.5 us  [the longest x8 11.6 us: ring_gather(): earlier.append(lax.ppermute(earlier[-1], axis, up))]
    unnamed x36 -> x61, local copies, waits for them, and re-layouts: 6.71 us -> 1.56 us
    all_to_all x1, starting transfers between devices: 7.38 us -> 3.62 us  [shards(): lax.all_to_all(outgoing, 'dom', split_axis=1, concat_axis=1, tiled=True)]
    select_n x3, other arithmetic: 0.01 us -> 1.32 us  [tile_terms(): picked = jnp.take(blocks, source, axis=1)]
    gather x1, local copies, waits for them, and re-layouts: 1.79 us -> 0.57 us  [shards(): hub_blocks = jnp.take(everyone, hub_owner * HOWN + order_rank, axis=1)]
    all_gather x1, blocking collectives: 6.51 us -> 5.63 us  [shards(): lax.all_gather(features, 'feat', axis=0, tiled=True)]
  transfers between devices with their start and end apart: 2 -> 16, of which waited for: 1 -> 7; matrix products, arithmetic and copies ran while one was open for 8% -> 11% of each run, Pallas kernels for 0% -> 0%
where the time goes in v1:
time: 81.7 us; the launch traced here: 81.3 us
  starting transfers between devices  35.7 us (44%)
  waiting for transfers between devices  15.5 us (19%)
  blocking collectives  11.3 us (14%)
  local copies, waits for them, and re-layouts  7.06 us (9%)
  matrix products  5.75 us (7%)
  other arithmetic  5.5 us (7%)
    ppermute x7, starting transfers between devices, ring_gather(): later.append(lax.ppermute(later[-1], axis, down))  31.1 us
    ppermute x8, waiting for transfers between devices, ring_gather(): earlier.append(lax.ppermute(earlier[-1], axis, up))  11.6 us
    all_gather x1, blocking collectives, shards(): lax.all_gather(aggregate, 'feat', axis=0, tiled=True)  5.64 us
    all_gather x1, blocking collectives, shards(): lax.all_gather(features, 'feat', axis=0, tiled=True)  5.63 us
    ppermute x7, waiting for transfers between devices, ring_gather(): later.append(lax.ppermute(later[-1], axis, down))  3.84 us
    all_to_all x1, starting transfers between devices, shards(): lax.all_to_all(outgoing, 'dom', split_axis=1, concat_axis=1, tiled=True)  3.62 us
    dot_general x3, matrix products, tile_terms(): jnp.einsum('fti,tr->fri', partial_value, onehot, precision=lax.Precision....  3.16 us
    gather x3, local copies, waits for them, and re-layouts, tile_terms(): picked = jnp.take(blocks, source, axis=1)  1.95 us
  transfers between devices with their start and end apart: 16, of which 7 were waited for; matrix products, arithmetic and copies ran while one was open for 11% of the time, Pallas kernels for 0%

profile of v1, /device:TPU:0, one launch (start us, length us, event | category | flops | bytes accessed | tf_op | source)
XLA Modules:
  0.0 81.3 jit_solution(16603174550052174920)
XLA Ops:
  0.0 0.9 %convert_reduce_fusion = s32[4]{0:T(128)S(1)} fusion(s32[4]{0:T(128)} %param.26), kind=kLoop, calls=%fused_computation.87 | loop fusion | flops 76 | bytes 32 | tf_op jit(solution)/shard_map/reduce_sum | solution.py:74
  0.9 0.7 compare_and_fusion.4
  1.6 0.8 multiply_reduce_fusion
  2.4 0.7 compare_select_fusion.2
  3.0 1.0 %copy.54 = bf16[128,512]{0,1:T(8,128)(2,1)S(1)} copy(bf16[128,512]{1,0:T(8,128)(2,1)} %param.22) | data formatting | bytes 262144 | tf_op args[0]
  4.1 0.9 %gather_fusion.4 = bf16[256,128]{1,0:T(8,128)(2,1)S(1)} fusion(bf16[128,512]{0,1:T(8,128)(2,1)S(1)} %copy.54, s32[1024]{0:T(1024)S(1)} %get-tuple-element.11), kind=kCustom, calls=%fused_computation.3.clone | custom fusion | bytes 132096 | tf_op jit(solution)/shard_map/jit(_take)/gather | solution.py:80
  5.7 5.1 %collective-permute-start.8 = (bf16[128,2,128]{2,0,1:T(8,128)(2,1)S(1)}, bf16[128,2,128]{2,0,1:T(8,128)(2,1)S(1)}, u32[]{:S(2)}, u32[]{:S(2)}) collective-permute-start(bf16[128,2,128]{2,0,1:T(8,128)(2,1)S(1)} %copy.61), channel_id=1, source_target_pairs={{0,30},{2,0},{4,2},{6,4},{8,6},{10,8},{12,10},{14,12},{16,14},{18,... | collective-permute-start | bytes 196616 | tf_op jit(solution)/shard_map/ppermute | solution.py:17
  10.7 0.8 reshape_squeeze.3
  11.5 0.7 compare_select_fusion.3
  12.2 0.9 %gather_fusion.3 = bf16[256,128]{1,0:T(8,128)(2,1)S(1)} fusion(bf16[128,512]{0,1:T(8,128)(2,1)S(1)} %copy.54, s32[1024]{0:T(1024)S(1)} %get-tuple-element.12), kind=kCustom, calls=%fused_computation.1.clone | custom fusion | bytes 132096 | tf_op jit(solution)/shard_map/jit(_take)/gather | solution.py:61
  13.1 0.7 fusion.21
  13.9 0.7 broadcast_multiply_fusion
  14.6 3.6 %all-to-all-start = ((bf16[128,16,16]{0,2,1:T(8,128)(2,1)}), bf16[128,16,16]{0,2,1:T(8,128)(2,1)S(1)}, u32[]{:S(2)}, u32[]{:S(2)}) async-start(bf16[128,16,16]{0,2,1:T(8,128)(2,1)} %broadcast_multiply_fusion), calls=%async_computation | async-start | bytes 131072 | tf_op jit(solution)/shard_map/all_to_all | solution.py:66
  19.7 1.1 %fusion.7 = f32[4,128,128]{2,0,1:T(4,128)S(1)} fusion(f32[128,16,128]{2,0,1:T(8,128)S(1)} %convolution_bitcast_fusion.2, s32[16]{0:T(128)S(1)} %copy-done.7), kind=kOutput, calls=%fused_computation.20 | convolution fusion | flops 12582976 | bytes 1310784 | tf_op jit(solution)/shard_map/fti,tr->fri/dot_general | solution.py:30
  21.3 6.0 %collective-permute-done.1 = bf16[128,2,128]{2,0,1:T(8,128)(2,1)S(1)} collective-permute-done((bf16[128,2,128]{2,0,1:T(8,128)(2,1)S(1)}, bf16[128,2,128]{2,0,1:T(8,128)(2,1)S(1)}, u32[]{:S(2)}, u32[]{:S(2)}) %collective-permute-start.1) | collective-permute-done | bytes 65568 | tf_op jit(solution)/shard_map/ppermute | solution.py:15
  27.3 4.5 %collective-permute-start.9 = (bf16[128,2,128]{2,0,1:T(8,128)(2,1)S(1)}, bf16[128,2,128]{2,0,1:T(8,128)(2,1)S(1)}, u32[]{:S(2)}, u32[]{:S(2)}) collective-permute-start(bf16[128,2,128]{2,0,1:T(8,128)(2,1)S(1)} %collective-permute-done.8), channel_id=1, source_target_pairs={{0,30},{2,0},{4,2},{6,4},{8,6},{10,8},{12,10},{14,12},{16,14},{18,... | collective-permute-start | bytes 196616 | tf_op jit(solution)/shard_map/ppermute | solution.py:17
  31.7 1.9 %collective-permute-done.2 = bf16[128,2,128]{2,0,1:T(8,128)(2,1)S(1)} collective-permute-done((bf16[128,2,128]{2,0,1:T(8,128)(2,1)S(1)}, bf16[128,2,128]{2,0,1:T(8,128)(2,1)S(1)}, u32[]{:S(2)}, u32[]{:S(2)}) %collective-permute-start.2) | collective-permute-done | bytes 65568 | tf_op jit(solution)/shard_map/ppermute | solution.py:15
  33.7 4.5 %collective-permute-start.10 = (bf16[128,2,128]{2,0,1:T(8,128)(2,1)S(1)}, bf16[128,2,128]{2,0,1:T(8,128)(2,1)S(1)}, u32[]{:S(2)}, u32[]{:S(2)}) collective-permute-start(bf16[128,2,128]{2,0,1:T(8,128)(2,1)S(1)} %collective-permute-done.9), channel_id=1, source_target_pairs={{0,30},{2,0},{4,2},{6,4},{8,6},{10,8},{12,10},{14,12},{16,14},{18,... | collective-permute-start | bytes 196616 | tf_op jit(solution)/shard_map/ppermute | solution.py:17
  38.1 1.9 %collective-permute-done.3 = bf16[128,2,128]{2,0,1:T(8,128)(2,1)S(1)} collective-permute-done((bf16[128,2,128]{2,0,1:T(8,128)(2,1)S(1)}, bf16[128,2,128]{2,0,1:T(8,128)(2,1)S(1)}, u32[]{:S(2)}, u32[]{:S(2)}) %collective-permute-start.3) | collective-permute-done | bytes 65568 | tf_op jit(solution)/shard_map/ppermute | solution.py:15
  40.0 4.5 %collective-permute-start.11 = (bf16[128,2,128]{2,0,1:T(8,128)(2,1)S(1)}, bf16[128,2,128]{2,0,1:T(8,128)(2,1)S(1)}, u32[]{:S(2)}, u32[]{:S(2)}) collective-permute-start(bf16[128,2,128]{2,0,1:T(8,128)(2,1)S(1)} %collective-permute-done.10), channel_id=1, source_target_pairs={{0,30},{2,0},{4,2},{6,4},{8,6},{10,8},{12,10},{14,12},{16,14},{18,... | collective-permute-start | bytes 196616 | tf_op jit(solution)/shard_map/ppermute | solution.py:17
  44.5 1.9 %collective-permute-done.4 = bf16[128,2,128]{2,0,1:T(8,128)(2,1)S(1)} collective-permute-done((bf16[128,2,128]{2,0,1:T(8,128)(2,1)S(1)}, bf16[128,2,128]{2,0,1:T(8,128)(2,1)S(1)}, u32[]{:S(2)}, u32[]{:S(2)}) %collective-permute-start.4) | collective-permute-done | bytes 65568 | tf_op jit(solution)/shard_map/ppermute | solution.py:15
  46.4 5.6 %all_gather.6 = bf16[256,512]{1,0:T(8,128)(2,1)S(1)} all-gather(bf16[128,512]{1,0:T(8,128)(2,1)S(1)} %copy-done.3), channel_id=1, replica_groups=mesh['dom'=16,'feat'=2] {'feat'}, dimensions={0}, use_global_device_ids=true | all-gather | bytes 393216 | tf_op jit(solution)/shard_map/all_gather | solution.py:94
  52.9 3.6 %collective-permute-start.12 = (bf16[128,2,128]{2,0,1:T(8,128)(2,1)S(1)}, bf16[128,2,128]{2,0,1:T(8,128)(2,1)S(1)}, u32[]{:S(2)}, u32[]{:S(2)}) collective-permute-start(bf16[128,2,128]{2,0,1:T(8,128)(2,1)S(1)} %collective-permute-done.11), channel_id=1, source_target_pairs={{0,30},{2,0},{4,2},{6,4},{8,6},{10,8},{12,10},{14,12},{16,14},{18,... | collective-permute-start | bytes 196616 | tf_op jit(solution)/shard_map/ppermute | solution.py:17
  57.0 1.4 %collective-permute-done.12 = bf16[128,2,128]{2,0,1:T(8,128)(2,1)S(1)} collective-permute-done((bf16[128,2,128]{2,0,1:T(8,128)(2,1)S(1)}, bf16[128,2,128]{2,0,1:T(8,128)(2,1)S(1)}, u32[]{:S(2)}, u32[]{:S(2)}) %collective-permute-start.12) | collective-permute-done | bytes 65568 | tf_op jit(solution)/shard_map/ppermute | solution.py:17
  58.4 4.5 %collective-permute-start.13 = (bf16[128,2,128]{2,0,1:T(8,128)(2,1)S(1)}, bf16[128,2,128]{2,0,1:T(8,128)(2,1)S(1)}, u32[]{:S(2)}, u32[]{:S(2)}) collective-permute-start(bf16[128,2,128]{2,0,1:T(8,128)(2,1)S(1)} %collective-permute-done.12), channel_id=1, source_target_pairs={{0,30},{2,0},{4,2},{6,4},{8,6},{10,8},{12,10},{14,12},{16,14},{18,... | collective-permute-start | bytes 196616 | tf_op jit(solution)/shard_map/ppermute | solution.py:17
  62.9 1.1 %convolution_add_fusion.1 = f32[4,128,128]{2,0,1:T(4,128)S(1)} fusion(f32[4,128,128]{2,0,1:T(4,128)S(1)} %fusion.7, f32[128,16,128]{2,0,1:T(8,128)S(1)} %convolution_bitcast_fusion.1, s32[16]{0:T(128)S(1)} %copy-done.8), kind=kOutput, calls=%fused_computation.10 | convolution fusion | flops 12648512 | bytes 1572928 | tf_op jit(solution)/shard_map/fti,tr->fri/dot_general | solution.py:30
  64.0 0.8 %collective-permute-done.13 = bf16[128,2,128]{2,0,1:T(8,128)(2,1)S(1)} collective-permute-done((bf16[128,2,128]{2,0,1:T(8,128)(2,1)S(1)}, bf16[128,2,128]{2,0,1:T(8,128)(2,1)S(1)}, u32[]{:S(2)}, u32[]{:S(2)}) %collective-permute-start.13) | collective-permute-done | bytes 65568 | tf_op jit(solution)/shard_map/ppermute | solution.py:17
  64.8 4.5 %collective-permute-start.14 = (bf16[128,2,128]{2,0,1:T(8,128)(2,1)S(1)}, bf16[128,2,128]{2,0,1:T(8,128)(2,1)S(1)}, u32[]{:S(2)}, u32[]{:S(2)}) collective-permute-start(bf16[128,2,128]{2,0,1:T(8,128)(2,1)S(1)} %collective-permute-done.13), channel_id=1, source_target_pairs={{0,30},{2,0},{4,2},{6,4},{8,6},{10,8},{12,10},{14,12},{16,14},{18,... | collective-permute-start | bytes 196616 | tf_op jit(solution)/shard_map/ppermute | solution.py:17
  69.5 1.6 %collective-permute-done.14 = bf16[128,2,128]{2,0,1:T(8,128)(2,1)S(1)} collective-permute-done((bf16[128,2,128]{2,0,1:T(8,128)(2,1)S(1)}, bf16[128,2,128]{2,0,1:T(8,128)(2,1)S(1)}, u32[]{:S(2)}, u32[]{:S(2)}) %collective-permute-start.14) | collective-permute-done | bytes 65568 | tf_op jit(solution)/shard_map/ppermute | solution.py:17
  73.5 1.1 %fusion.3 = bf16[4,128,128]{2,0,1:T(4,128)(2,1)S(1)} fusion(f32[4,128,128]{2,0,1:T(4,128)S(1)} %convolution_add_fusion.1, f32[128,16,128]{2,0,1:T(8,128)S(1)} %convolution_bitcast_fusion, f32[4,128]{1,0:T(4,128)S(1)} %convert_bitcast_fusion, s32[16]{0:T(128)S(1)} %copy-done.13), kind=kOutput, calls=%fused_computation.16 | convolution fusion | flops 12779584 | bytes 1443904 | tf_op jit(solution)/shard_map/fti,tr->fri/dot_general | solution.py:30
  74.6 5.6 %all_gather.7 = bf16[256,512]{1,0:T(8,128)(2,1)S(1)} all-gather(bf16[128,512]{1,0:T(8,128)(2,1)S(1)} %bitcast.56), channel_id=1, replica_groups=mesh['dom'=16,'feat'=2] {'feat'}, dimensions={0}, use_global_device_ids=true | all-gather | bytes 393216 | tf_op jit(solution)/shard_map/all_gather | solution.py:99
  80.5 0.9 %fusion.4 = bf16[128,512]{1,0:T(8,128)(2,1)} fusion(f32[128,512]{1,0:T(8,128)S(1)} %convolution_bitcast_fusion.3, bf16[128,256]{1,0:T(8,128)(2,1)S(1)} %copy-done.5, bf16[256,512]{1,0:T(8,128)(2,1)S(1)} %all_gather.6, f32[128]{0:T(128)S(1)} %copy-done.9), kind=kOutput, calls=%fused_computation.17 | convolution fusion | flops 33816576 | bytes 721408 | tf_op jit(solution)/shard_map/dot_general | solution.py:92
  (107 shorter events, 6.7 us)
Async XLA Ops:
  0.0 19.1 %copy-start = (bf16[16,128,128]{2,1,0:T(8,128)(2,1)S(1)}, bf16[16,128,128]{2,1,0:T(8,128)(2,1)}, u32[]{:S(2)}) copy-start(bf16[16,128,128]{2,1,0:T(8,128)(2,1)} %param.30) | copy-start | bytes 1572868
  0.0 18.3 %copy-start.10 = (s32[16]{0:T(128)S(1)}, s32[16]{0:T(128)}, u32[]{:S(2)}) copy-start(s32[16]{0:T(128)} %param.29) | copy-start | bytes 196
  0.0 18.4 %copy-start.6 = (s32[512]{0:T(512)S(1)}, s32[512]{0:T(512)}, u32[]{:S(2)}) copy-start(s32[512]{0:T(512)} %param.23) | copy-start | bytes 6148
  5.2 15.6 %collective-permute-start = (bf16[128,2,128]{2,0,1:T(8,128)(2,1)S(1)}, bf16[128,2,128]{2,0,1:T(8,128)(2,1)S(1)}, u32[]{:S(2)}, u32[]{:S(2)}) collective-permute-start(bf16[128,2,128]{2,0,1:T(8,128)(2,1)S(1)} %copy.61), channel_id=1, source_target_pairs={{0,2},{2,4},{4,6},{6,8},{8,10},{10,12},{12,14},{14,16},{16,18},{18... | collective-permute-start | bytes 196616 | tf_op jit(solution)/shard_map/ppermute | solution.py:15
  5.7 21.6 %collective-permute-start.8 = (bf16[128,2,128]{2,0,1:T(8,128)(2,1)S(1)}, bf16[128,2,128]{2,0,1:T(8,128)(2,1)S(1)}, u32[]{:S(2)}, u32[]{:S(2)}) collective-permute-start(bf16[128,2,128]{2,0,1:T(8,128)(2,1)S(1)} %copy.61), channel_id=1, source_target_pairs={{0,30},{2,0},{4,2},{6,4},{8,6},{10,8},{12,10},{14,12},{16,14},{18,... | collective-permute-start | bytes 196616 | tf_op jit(solution)/shard_map/ppermute | solution.py:17
  12.2 7.5 %copy-start.7 = (s32[16]{0:T(128)S(1)}, s32[16]{0:T(128)}, u32[]{:S(2)}) copy-start(s32[16]{0:T(128)} %param.28) | copy-start | bytes 196
  14.6 37.4 %all-to-all-start = ((bf16[128,16,16]{0,2,1:T(8,128)(2,1)}), bf16[128,16,16]{0,2,1:T(8,128)(2,1)S(1)}, u32[]{:S(2)}, u32[]{:S(2)}) async-start(bf16[128,16,16]{0,2,1:T(8,128)(2,1)} %broadcast_multiply_fusion), calls=%async_computation | async-start | bytes 131072 | tf_op jit(solution)/shard_map/all_to_all | solution.py:66
  18.4 2.3 %copy-start.11 = (s32[16]{0:T(128)S(1)}, s32[16]{0:T(128)}, u32[]{:S(2)}) copy-start(s32[16]{0:T(128)} %param.35) | copy-start | bytes 196
  18.4 2.8 %copy-start.12 = (s32[16]{0:T(128)S(1)}, s32[16]{0:T(128)}, u32[]{:S(2)}) copy-start(s32[16]{0:T(128)} %param.32) | copy-start | bytes 196
  18.5 28.0 %copy-start.3 = (bf16[128,512]{1,0:T(8,128)(2,1)S(1)}, bf16[128,512]{1,0:T(8,128)(2,1)}, u32[]{:S(2)}) copy-start(bf16[128,512]{1,0:T(8,128)(2,1)} %param.22) | copy-start | bytes 393220
  19.1 37.4 %copy-start.1 = (bf16[16,128,128]{2,1,0:T(8,128)(2,1)S(1)}, bf16[16,128,128]{2,1,0:T(8,128)(2,1)}, u32[]{:S(2)}) copy-start(bf16[16,128,128]{2,1,0:T(8,128)(2,1)} %param.33) | copy-start | bytes 1572868
  20.8 42.1 %copy-start.8 = (s32[16]{0:T(128)S(1)}, s32[16]{0:T(128)}, u32[]{:S(2)}) copy-start(s32[16]{0:T(128)} %param.31) | copy-start | bytes 196
  20.8 6.4 %collective-permute-start.1 = (bf16[128,2,128]{2,0,1:T(8,128)(2,1)S(1)}, bf16[128,2,128]{2,0,1:T(8,128)(2,1)S(1)}, u32[]{:S(2)}, u32[]{:S(2)}) collective-permute-start(bf16[128,2,128]{2,0,1:T(8,128)(2,1)S(1)} %collective-permute-done), channel_id=1, source_target_pairs={{0,2},{2,4},{4,6},{6,8},{8,10},{10,12},{12,14},{14,16},{16,18},{18... | collective-permute-start | bytes 196616 | tf_op jit(solution)/shard_map/ppermute | solution.py:15
  27.2 6.4 %collective-permute-start.2 = (bf16[128,2,128]{2,0,1:T(8,128)(2,1)S(1)}, bf16[128,2,128]{2,0,1:T(8,128)(2,1)S(1)}, u32[]{:S(2)}, u32[]{:S(2)}) collective-permute-start(bf16[128,2,128]{2,0,1:T(8,128)(2,1)S(1)} %collective-permute-done.1), channel_id=1, source_target_pairs={{0,2},{2,4},{4,6},{6,8},{8,10},{10,12},{12,14},{14,16},{16,18},{18... | collective-permute-start | bytes 196616 | tf_op jit(solution)/shard_map/ppermute | solution.py:15
  27.3 6.4 %collective-permute-start.9 = (bf16[128,2,128]{2,0,1:T(8,128)(2,1)S(1)}, bf16[128,2,128]{2,0,1:T(8,128)(2,1)S(1)}, u32[]{:S(2)}, u32[]{:S(2)}) collective-permute-start(bf16[128,2,128]{2,0,1:T(8,128)(2,1)S(1)} %collective-permute-done.8), channel_id=1, source_target_pairs={{0,30},{2,0},{4,2},{6,4},{8,6},{10,8},{12,10},{14,12},{16,14},{18,... | collective-permute-start | bytes 196616 | tf_op jit(solution)/shard_map/ppermute | solution.py:17
  33.6 6.4 %collective-permute-start.3 = (bf16[128,2,128]{2,0,1:T(8,128)(2,1)S(1)}, bf16[128,2,128]{2,0,1:T(8,128)(2,1)S(1)}, u32[]{:S(2)}, u32[]{:S(2)}) collective-permute-start(bf16[128,2,128]{2,0,1:T(8,128)(2,1)S(1)} %collective-permute-done.2), channel_id=1, source_target_pairs={{0,2},{2,4},{4,6},{6,8},{8,10},{10,12},{12,14},{14,16},{16,18},{18... | collective-permute-start | bytes 196616 | tf_op jit(solution)/shard_map/ppermute | solution.py:15
  33.7 6.4 %collective-permute-start.10 = (bf16[128,2,128]{2,0,1:T(8,128)(2,1)S(1)}, bf16[128,2,128]{2,0,1:T(8,128)(2,1)S(1)}, u32[]{:S(2)}, u32[]{:S(2)}) collective-permute-start(bf16[128,2,128]{2,0,1:T(8,128)(2,1)S(1)} %collective-permute-done.9), channel_id=1, source_target_pairs={{0,30},{2,0},{4,2},{6,4},{8,6},{10,8},{12,10},{14,12},{16,14},{18,... | collective-permute-start | bytes 196616 | tf_op jit(solution)/shard_map/ppermute | solution.py:17
  40.0 6.4 %collective-permute-start.4 = (bf16[128,2,128]{2,0,1:T(8,128)(2,1)S(1)}, bf16[128,2,128]{2,0,1:T(8,128)(2,1)S(1)}, u32[]{:S(2)}, u32[]{:S(2)}) collective-permute-start(bf16[128,2,128]{2,0,1:T(8,128)(2,1)S(1)} %collective-permute-done.3), channel_id=1, source_target_pairs={{0,2},{2,4},{4,6},{6,8},{8,10},{10,12},{12,14},{14,16},{16,18},{18... | collective-permute-start | bytes 196616 | tf_op jit(solution)/shard_map/ppermute | solution.py:15
  40.0 12.8 %collective-permute-start.11 = (bf16[128,2,128]{2,0,1:T(8,128)(2,1)S(1)}, bf16[128,2,128]{2,0,1:T(8,128)(2,1)S(1)}, u32[]{:S(2)}, u32[]{:S(2)}) collective-permute-start(bf16[128,2,128]{2,0,1:T(8,128)(2,1)S(1)} %collective-permute-done.10), channel_id=1, source_target_pairs={{0,30},{2,0},{4,2},{6,4},{8,6},{10,8},{12,10},{14,12},{16,14},{18,... | collective-permute-start | bytes 196616 | tf_op jit(solution)/shard_map/ppermute | solution.py:17
  46.4 10.1 %collective-permute-start.5 = (bf16[128,2,128]{2,0,1:T(8,128)(2,1)S(1)}, bf16[128,2,128]{2,0,1:T(8,128)(2,1)S(1)}, u32[]{:S(2)}, u32[]{:S(2)}) collective-permute-start(bf16[128,2,128]{2,0,1:T(8,128)(2,1)S(1)} %collective-permute-done.4), channel_id=1, source_target_pairs={{0,2},{2,4},{4,6},{6,8},{8,10},{10,12},{12,14},{14,16},{16,18},{18... | collective-permute-start | bytes 196616 | tf_op jit(solution)/shard_map/ppermute | solution.py:15
  52.9 5.5 %collective-permute-start.12 = (bf16[128,2,128]{2,0,1:T(8,128)(2,1)S(1)}, bf16[128,2,128]{2,0,1:T(8,128)(2,1)S(1)}, u32[]{:S(2)}, u32[]{:S(2)}) collective-permute-start(bf16[128,2,128]{2,0,1:T(8,128)(2,1)S(1)} %collective-permute-done.11), channel_id=1, source_target_pairs={{0,30},{2,0},{4,2},{6,4},{8,6},{10,8},{12,10},{14,12},{16,14},{18,... | collective-permute-start | bytes 196616 | tf_op jit(solution)/shard_map/ppermute | solution.py:17
  56.5 6.4 %collective-permute-start.6 = (bf16[128,2,128]{2,0,1:T(8,128)(2,1)S(1)}, bf16[128,2,128]{2,0,1:T(8,128)(2,1)S(1)}, u32[]{:S(2)}, u32[]{:S(2)}) collective-permute-start(bf16[128,2,128]{2,0,1:T(8,128)(2,1)S(1)} %collective-permute-done.5), channel_id=1, source_target_pairs={{0,2},{2,4},{4,6},{6,8},{8,10},{10,12},{12,14},{14,16},{16,18},{18... | collective-permute-start | bytes 196616 | tf_op jit(solution)/shard_map/ppermute | solution.py:15
  58.4 6.4 %collective-permute-start.13 = (bf16[128,2,128]{2,0,1:T(8,128)(2,1)S(1)}, bf16[128,2,128]{2,0,1:T(8,128)(2,1)S(1)}, u32[]{:S(2)}, u32[]{:S(2)}) collective-permute-start(bf16[128,2,128]{2,0,1:T(8,128)(2,1)S(1)} %collective-permute-done.12), channel_id=1, source_target_pairs={{0,30},{2,0},{4,2},{6,4},{8,6},{10,8},{12,10},{14,12},{16,14},{18,... | collective-permute-start | bytes 196616 | tf_op jit(solution)/shard_map/ppermute | solution.py:17
  62.9 6.4 %collective-permute-start.7 = (bf16[128,2,128]{2,0,1:T(8,128)(2,1)S(1)}, bf16[128,2,128]{2,0,1:T(8,128)(2,1)S(1)}, u32[]{:S(2)}, u32[]{:S(2)}) collective-permute-start(bf16[128,2,128]{2,0,1:T(8,128)(2,1)S(1)} %collective-permute-done.6), channel_id=1, source_target_pairs={{0,2},{2,4},{4,6},{6,8},{8,10},{10,12},{12,14},{14,16},{16,18},{18... | collective-permute-start | bytes 196616 | tf_op jit(solution)/shard_map/ppermute | solution.py:15
  64.8 6.4 %collective-permute-start.14 = (bf16[128,2,128]{2,0,1:T(8,128)(2,1)S(1)}, bf16[128,2,128]{2,0,1:T(8,128)(2,1)S(1)}, u32[]{:S(2)}, u32[]{:S(2)}) collective-permute-start(bf16[128,2,128]{2,0,1:T(8,128)(2,1)S(1)} %collective-permute-done.13), channel_id=1, source_target_pairs={{0,30},{2,0},{4,2},{6,4},{8,6},{10,8},{12,10},{14,12},{16,14},{18,... | collective-permute-start | bytes 196616 | tf_op jit(solution)/shard_map/ppermute | solution.py:17
  71.4 1.5 %copy-start.2 = (bf16[16,128,128]{2,1,0:T(8,128)(2,1)S(1)}, bf16[16,128,128]{2,1,0:T(8,128)(2,1)}, u32[]{:S(2)}) copy-start(bf16[16,128,128]{2,1,0:T(8,128)(2,1)} %param.36) | copy-start | bytes 1572868
  71.6 1.9 %copy-start.13 = (s32[16]{0:T(128)S(1)}, s32[16]{0:T(128)}, u32[]{:S(2)}) copy-start(s32[16]{0:T(128)} %param.34) | copy-start | bytes 196
  73.0 7.3 %copy-start.4 = (bf16[128,256]{1,0:T(8,128)(2,1)S(1)}, bf16[128,256]{1,0:T(8,128)(2,1)}, u32[]{:S(2)}) copy-start(bf16[128,256]{1,0:T(8,128)(2,1)} %param.38) | copy-start | bytes 196612
  73.5 7.0 %copy-start.5 = (bf16[128,256]{1,0:T(8,128)(2,1)S(1)}, bf16[128,256]{1,0:T(8,128)(2,1)}, u32[]{:S(2)}) copy-start(bf16[128,256]{1,0:T(8,128)(2,1)} %param.37) | copy-start | bytes 196612
  73.5 7.0 %copy-start.9 = (f32[128]{0:T(128)S(1)}, f32[128]{0:T(128)}, u32[]{:S(2)}) copy-start(f32[128]{0:T(128)} %param.39) | copy-start | bytes 1540
